TPU v7x, 256 devices: a whole 4x4x8 slice. The times are simulated.
256 devices in a mesh: gx: 4 (over x), gy: 8 (over z_lo, core), gz: 8 (over z_hi, y).
Axes of the slice: x: 4, y: 4, z: 8 (z_hi: 2, z_lo: 4; z = z_hi * 4 + z_lo), core: 2. Of those that a mesh axis runs over, the one named last changes fastest.
Arguments:
- activations: bfloat16 [64, 32, 64, 1024], P(None, 'gx', 'gy', 'gz'), may hold values from -6 to 6
- preact: bfloat16 [64, 32, 64, 1024], P(None, 'gx', 'gy', 'gz'), may hold values from -6 to 6
- upstream: bfloat16 [64, 32, 64, 1024], P(None, 'gx', 'gy', 'gz'), may hold values from -6 to 6
- master: float32 [110592], P(('gx', 'gy', 'gz')), may hold values from -0.15625 to 0.15625
- first_moment: float32 [110592], P(('gx', 'gy', 'gz')), may hold values from -4 to 4
- second_moment: float32 [110592], P(('gx', 'gy', 'gz')), may hold values from 0.05 to 2
Outputs:
- grad_input: bfloat16 [64, 32, 64, 1024], P(None, 'gx', 'gy', 'gz')
- weight_grad: float32 [110592], P(('gx', 'gy', 'gz'))
- new_master: float32 [110592], P(('gx', 'gy', 'gz'))
- new_first: float32 [110592], P(('gx', 'gy', 'gz'))
- new_second: float32 [110592], P(('gx', 'gy', 'gz'))
All inputs are finite; a program needn't handle non-finite values.
Results may differ from a plain program's by a relative error of at most 0.0049.
Values may be sent and summed in bfloat16 or wider, within the bound.
A program may use at most 64 MiB of HBM per device.

v0:
```python
import math

import jax
import jax.numpy as jnp
from jax import lax
from jax.sharding import PartitionSpec as P


def padded_2(block, sides, width):
    for axis, dim in sides:
        count = lax.axis_size(axis)
        forward = [(i, i + 1) for i in range(count - 1)]
        backward = [(target, source) for source, target in forward]
        low = lax.ppermute(
            lax.slice_in_dim(block, block.shape[dim] - width, None, axis=dim), axis, forward
        )
        high = lax.ppermute(lax.slice_in_dim(block, 0, width, axis=dim), axis, backward)
        block = jnp.concatenate([low, block, high], axis=dim)
    return block


def local(activations, preact, upstream, master, first_moment, second_moment):
    channels = activations.shape[0]
    size_x, size_y, size_z = (activations.shape[1], activations.shape[2], activations.shape[3])
    pre_grad = jnp.where(preact > 0, upstream, jnp.zeros_like(upstream))
    stacked = jnp.stack([activations, pre_grad])
    padded = padded_2(stacked, (("gx", 2), ("gy", 3), ("gz", 4)), 1)
    padded_input = padded[0]
    padded_grad = padded[1]
    kernel_flat = lax.all_gather(
        master.astype(jnp.bfloat16), ("gx", "gy", "gz"), axis=0, tiled=True
    )
    kernel = kernel_flat.reshape(channels, channels, 3, 3, 3)
    flipped = jnp.transpose(kernel, (1, 0, 2, 3, 4))[:, :, ::-1, ::-1, ::-1]
    conv_out = lax.conv_general_dilated(
        padded_grad[None],
        flipped,
        (1, 1, 1),
        "VALID",
        dimension_numbers=("NCDHW", "OIDHW", "NCDHW"),
        preferred_element_type=jnp.float32,
    )
    grad_input = conv_out[0].astype(jnp.bfloat16)
    tap_terms = []
    for shift_x in range(3):
        for shift_y in range(3):
            for shift_z in range(3):
                window = padded_input[
                    :,
                    shift_x : shift_x + size_x,
                    shift_y : shift_y + size_y,
                    shift_z : shift_z + size_z,
                ]
                tap_terms.append(
                    lax.dot_general(
                        pre_grad,
                        window,
                        (((1, 2, 3), (1, 2, 3)), ((), ())),
                        preferred_element_type=jnp.float32,
                    )
                )
    voxels = (
        size_x * size_y * size_z * lax.axis_size("gx") * lax.axis_size("gy") * lax.axis_size("gz")
    )
    flattened = jnp.stack(tap_terms, axis=-1).reshape(-1) / math.sqrt(voxels)
    weight_grad = lax.psum_scatter(flattened, ("gx", "gy", "gz"), scatter_dimension=0, tiled=True)
    new_first = 0.9 * first_moment + 0.1 * weight_grad
    new_second = 0.999 * second_moment + 0.001 * weight_grad * weight_grad
    corr_first = 1.0 - (0.9**10) ** 10
    corr_second = 1.0 - (0.999**10) ** 10
    update = new_first / corr_first / (jnp.sqrt(new_second / corr_second) + 1e-08) + 0.01 * master
    new_master = master - 0.05 * update
    return (grad_input, weight_grad, new_master, new_first, new_second)


def solution(mesh):
    in_specs = (
        P(None, "gx", "gy", "gz"),
        P(None, "gx", "gy", "gz"),
        P(None, "gx", "gy", "gz"),
        P(("gx", "gy", "gz")),
        P(("gx", "gy", "gz")),
        P(("gx", "gy", "gz")),
    )
    out_specs = (
        P(None, "gx", "gy", "gz"),
        P(("gx", "gy", "gz")),
        P(("gx", "gy", "gz")),
        P(("gx", "gy", "gz")),
        P(("gx", "gy", "gz")),
    )
    return jax.shard_map(local, mesh=mesh, in_specs=in_specs, out_specs=out_specs, check_vma=False)
```

profile of v0, /device:TPU:1, one launch (start us, length us, event | category | flops | bytes accessed | tf_op | source)
XLA Modules:
  0.0 660.4 jit_solution(10823654515251285457)
XLA Ops:
  7.2 1.9 copy.69
  9.1 3.3 compare_select_fusion
  12.4 3.9 collective-permute-start
  16.4 1.3 collective-permute-start.1
  17.7 3.7 collective-permute-done
  21.4 3.8 collective-permute-done.1
  25.3 5.2 collective-permute-start.2
  30.6 1.9 collective-permute-start.3
  32.5 2.1 collective-permute-done.2
  34.6 4.4 collective-permute-done.3
  39.7 4.4 fusion.70
  44.0 3.5 copy.27
  47.6 3.2 collective-permute-start.4
  50.8 3.5 copy.28
  54.3 1.3 collective-permute-start.5
  55.6 3.2 copy.29
  59.2 3.0 copy.30
  62.2 9.4 %pad_maximum_fusion = bf16[2,64,10,10,130]{4,1,3,2,0:T(8,128)(2,1)S(1)} fusion(bf16[2,64,10,10,1]{4,1,3,2,0:T(8,128)(2,1)} %copy.30, bf16[2,64,10,1,128]{4,1,3,2,0:T(8,128)(2,1)S(1)} %collective-permute-done.3, bf16[2,64,1,8,128]{4,1,3,2,0:T(8,128)(2,1)S(1)} %collective-permute-done.1, bf16[1,64,8,8,128]{4,1,3,2,0:T(8,128)(2,1)S(1)} %bitcast.269, ...), kind=kLoop, calls=%fused_computation.2 | loop fusion | flops 26624000 | bytes 6656000 | tf_op jit(solution)/shard_map/concatenate | solution.py:18
  71.7 2.7 slice_bitcast_fusion
  89.1 2.8 div.25
  92.0 261.3 %all-reduce.7.cloned.1.call-done = f32[110592]{0:T(1024)} async-done(((f32[110592]{0:T(1024)}), f32[110592]{0:T(1024)}) %all-reduce.7.cloned.1.call-update) | async-done | bytes 442384
  353.3 1.4 multiply_subtract_fusion
  355.7 4.5 copy.65
  360.2 2.5 pad.clone
  362.7 7.1 %reshape.20 = bf16[64,10,10,1,8,17]{0,5,4,2,1,3:T(8,128)(2,1)} reshape(bf16[64,10,10,1,136]{0,4,2,1,3:T(8,128)(2,1)} %pad.clone) | data formatting | bytes 3481600 | tf_op jit(solution)/shard_map/conv_general_dilated | solution.py:35
  369.8 3.0 copy.33
  372.8 0.9 slice.145
  373.7 236.1 %all-reduce.5.cloned.1.call-done = bf16[110592]{0:T(1024)(128)(2,1)} async-done(((bf16[110592]{0:T(1024)(128)(2,1)}), bf16[110592]{0:T(1024)(128)(2,1)}) %all-reduce.5.cloned.1.call-update) | async-done | bytes 221200
  609.8 12.2 %reshape.17 = bf16[64,64,3,3,3]{4,3,2,1,0:T(4,128)(2,1)} reshape(bf16[110592]{0:T(1024)(128)(2,1)} %all-reduce.5.cloned.1.call-done) | data formatting | bytes 442368 | tf_op jit(solution)/shard_map/reshape | solution.py:33
  622.1 18.3 %copy.34 = bf16[64,64,3,3,3]{1,0,4,3,2:T(8,128)(2,1)} copy(bf16[64,64,3,3,3]{4,3,2,1,0:T(4,128)(2,1)} %reshape.17) | data formatting | bytes 442368 | tf_op jit(solution)/shard_map/reshape | solution.py:33
  640.3 9.7 %select_convert_fusion = bf16[8,8,8,17,64]{4,2,3,1,0:T(8,128)(2,1)S(1)} fusion(pred[8,17]{0,1:T(8,128)(4,1)S(1)} %copy-done.4, bf16[64,64,3,3,3]{1,0,4,3,2:T(8,128)(2,1)} %copy.34, bf16[64,10,10,1,7,2]{0,4,5,2,1,3:T(8,128)(2,1)} %slice.145, bf16[64,10,10,1,8,17]{0,4,5,2,1,3:T(8,128)(2,1)S(1)} %copy.33), kind=kOutput, calls=%fused_computation.3 | convolution fusion | flops 1932136448 | bytes 3255432 | tf_op jit(solution)/shard_map/conv_general_dilated | solution.py:35
  650.5 3.0 copy.37
  (52 shorter events, 17.2 us)
Async XLA Ops:
  7.2 346.2 %all-reduce.7.cloned.1.call-start = ((), (), s32[]{:S(2)}) async-start(), calls=%async_computation.1 | async-start | bytes 884736
  12.4 8.9 %collective-permute-start = (bf16[2,64,1,8,128]{4,1,3,2,0:T(8,128)(2,1)S(1)}, bf16[2,64,1,8,128]{4,1,3,2,0:T(8,128)(2,1)S(1)}, u32[]{:S(2)}, u32[]{:S(2)}) collective-permute-start(bf16[2,64,1,8,128]{4,1,3,2,0:T(8,128)(2,1)S(1)} %get-tuple-element.25), channel_id=1, source_target_pairs={{0,64},{64,128},{128,192},{1,65},{65,129},{129,193},{2,66},{66,130... | collective-permute-start | bytes 786440 | tf_op jit(solution)/shard_map/ppermute | solution.py:14
  16.4 8.8 %collective-permute-start.1 = (bf16[2,64,1,8,128]{4,1,3,2,0:T(8,128)(2,1)S(1)}, bf16[2,64,1,8,128]{4,1,3,2,0:T(8,128)(2,1)S(1)}, u32[]{:S(2)}, u32[]{:S(2)}) collective-permute-start(bf16[2,64,1,8,128]{4,1,3,2,0:T(8,128)(2,1)S(1)} %get-tuple-element.26), channel_id=1, source_target_pairs={{64,0},{128,64},{192,128},{65,1},{129,65},{193,129},{66,2},{130,66... | collective-permute-start | bytes 786440 | tf_op jit(solution)/shard_map/ppermute | solution.py:17
  25.3 9.2 %collective-permute-start.2 = (bf16[2,64,10,1,128]{4,1,3,2,0:T(8,128)(2,1)S(1)}, bf16[2,64,10,1,128]{4,1,3,2,0:T(8,128)(2,1)S(1)}, u32[]{:S(2)}, u32[]{:S(2)}) collective-permute-start(bf16[2,64,10,1,128]{4,1,3,2,0:T(8,128)(2,1)S(1)} %get-tuple-element.23), channel_id=1, source_target_pairs={{0,8},{8,16},{16,24},{24,32},{32,40},{40,48},{48,56},{1,9},{9,17},... | collective-permute-start | bytes 983048 | tf_op jit(solution)/shard_map/ppermute | solution.py:14
  30.6 8.4 %collective-permute-start.3 = (bf16[2,64,10,1,128]{4,1,3,2,0:T(8,128)(2,1)S(1)}, bf16[2,64,10,1,128]{4,1,3,2,0:T(8,128)(2,1)S(1)}, u32[]{:S(2)}, u32[]{:S(2)}) collective-permute-start(bf16[2,64,10,1,128]{4,1,3,2,0:T(8,128)(2,1)S(1)} %get-tuple-element.24), channel_id=1, source_target_pairs={{8,0},{16,8},{24,16},{32,24},{40,32},{48,40},{56,48},{9,1},{17,9},... | collective-permute-start | bytes 983048 | tf_op jit(solution)/shard_map/ppermute | solution.py:17
  47.6 8.1 %collective-permute-start.4 = (bf16[2,64,10,10,1]{1,0,4,3,2:T(2,128)(2,1)S(1)}, bf16[2,64,10,10,1]{1,0,4,3,2:T(2,128)(2,1)S(1)}, u32[]{:S(2)}, u32[]{:S(2)}) collective-permute-start(bf16[2,64,10,10,1]{1,0,4,3,2:T(2,128)(2,1)S(1)} %copy.27), channel_id=1, source_target_pairs={{0,1},{1,2},{2,3},{3,4},{4,5},{5,6},{6,7},{8,9},{9,10},{10,11},{11... | collective-permute-start | bytes 76808 | tf_op jit(solution)/shard_map/ppermute | solution.py:14
  54.3 4.9 collective-permute-start.5
  88.4 264.9 %copy-start.1 = (f32[432]{0:T(512)S(1)}, f32[432]{0:T(512)}, u32[]{:S(2)}) copy-start(f32[432]{0:T(512)} %param.9) | copy-start | bytes 5188
  88.4 264.9 %copy-start.2 = (f32[432]{0:T(512)S(1)}, f32[432]{0:T(512)}, u32[]{:S(2)}) copy-start(f32[432]{0:T(512)} %param.10) | copy-start | bytes 5188
  88.4 264.9 %copy-start.3 = (f32[432]{0:T(512)S(1)}, f32[432]{0:T(512)}, u32[]{:S(2)}) copy-start(f32[432]{0:T(512)} %param.11) | copy-start | bytes 5188
  91.9 517.9 %all-reduce.5.cloned.1.call-start = ((), (), s32[]{:S(2)}) async-start(), calls=%async_computation | async-start | bytes 442368
  355.0 0.7 copy-start
  622.1 18.3 %copy-start.4 = (pred[8,17]{0,1:T(8,128)(4,1)S(1)}, pred[8,17]{0,1:T(8,128)(4,1)}, u32[]{:S(2)}) copy-start(pred[8,17]{0,1:T(8,128)(4,1)} %constant.32) | copy-start | bytes 412
Sparse Core Ops, SparseCore 0:
  92.0 261.2 all-reduce.6
  359.4 250.3 all-reduce.4
where the time goes:
time: 662 us; the launch traced here: 660 us
  waiting for transfers between devices  512 us (77%)
  local copies, waits for them, and re-layouts  78.7 us (12%)
  matrix products  23.4 us (4%)
  starting transfers between devices  17 us (3%)
  other arithmetic  15 us (2%)
  between operations  14.5 us (2%)
    unnamed x4, waiting for transfers between devices  497 us
    reshape x2, local copies, waits for them, and re-layouts, local(): kernel = kernel_flat.reshape(channels, channels, 3, 3, 3)  30.5 us
    dot_general x27, matrix products, local(): lax.dot_general(pre_grad, window, (((1, 2, 3), (1, 2, 3)), ((), ())), pre...  13.7 us
  transfers between devices with their start and end apart: 8, of which 7 were waited for; matrix products, arithmetic and copies ran while one was open for 4% of the time, Pallas kernels for 0%

commit v1 on v0

v1 whole, which is shorter than its diff:
```python
import functools
import math

import jax
import jax.numpy as jnp
from jax import lax
from jax.experimental import pallas as pl
from jax.experimental.pallas import tpu as pltpu
from jax.sharding import PartitionSpec as P

MESH = pl.DeviceIdType.MESH
BF, F32 = jnp.bfloat16, jnp.float32
GX, GY, GZ = 4, 8, 8
C = 64
SX, SY, SZ = 8, 8, 128
ROW = SY * SZ
PROW = (SY + 2) * SZ
DIRS = [(1, 0), (-1, 0), (0, 1), (0, -1), (1, 1), (1, -1), (-1, 1), (-1, -1)]
NT = (((1,), (1,)), ((), ()))
NN = (((1,), (0,)), ((), ()))


def dot(a, b, dims):
    return lax.dot_general(a, b, dims, preferred_element_type=F32)


def lanes(shape):
    return lax.broadcasted_iota(jnp.int32, shape, 1)


def kernel(
    pg_ref, x_ref, wp_ref, out_ref, wg_ref,
    pg3, x12, pack, spread, gacc, dfull, acc,
    zsend, zrecv, xface, xroll,
    az, ax, wf, wk, wl,
    sx, rx, ef, ff, sy, ry, szf, rz,
    halo_s, halo_r, z_s, z_r, az_s, az_r, ay_s, ay_r, ax_s, ax_r,
    rx_s, rx_r, ry_s, ry_r, rz_s, rz_r,
):
    gx, gy, gz = lax.axis_index("gx"), lax.axis_index("gy"), lax.axis_index("gz")

    def send(src, dst, ss, rs, dev):
        return pltpu.make_async_remote_copy(
            src_ref=src, dst_ref=dst, send_sem=ss, recv_sem=rs, device_id=dev, device_id_type=MESH
        )

    barrier = pltpu.get_barrier_semaphore()
    for k in range(1, GX):
        pl.semaphore_signal(barrier, inc=1, device_id={"gx": lax.rem(gx + k, GX)}, device_id_type=MESH)
    for k in range(1, GY):
        pl.semaphore_signal(barrier, inc=1, device_id={"gy": lax.rem(gy + k, GY)}, device_id_type=MESH)
    for k in range(1, GZ):
        pl.semaphore_signal(barrier, inc=1, device_id={"gz": lax.rem(gz + k, GZ)}, device_id_type=MESH)
    for dx, dy in DIRS[4:]:
        pl.semaphore_signal(
            barrier,
            inc=1,
            device_id={"gx": lax.rem(gx + dx + GX, GX), "gy": lax.rem(gy + dy + GY, GY)},
            device_id_type=MESH,
        )

    pg3[1 : SX + 1, C : 2 * C, SZ : SZ + ROW] = pg_ref[...]
    x12[0 : 2 * C, :] = jnp.zeros((2 * C, ROW), BF)
    x12[(SX + 2) * C :, :] = jnp.zeros((2 * C, ROW), BF)
    for i in range(SX):
        x12[(i + 2) * C : (i + 3) * C, :] = x_ref[i]

    def where(d):
        sxd, syd = d
        if sxd == 1:
            sp, dp = pl.ds(SX - 1, 1), pl.ds(0, 1)
        elif sxd == -1:
            sp, dp = pl.ds(0, 1), pl.ds(SX + 1, 1)
        else:
            sp, dp = pl.ds(0, SX), pl.ds(1, SX)
        if syd == 1:
            sl, dl = pl.ds(ROW - SZ, SZ), pl.ds(0, SZ)
        elif syd == -1:
            sl, dl = pl.ds(0, SZ), pl.ds(PROW - SZ, SZ)
        else:
            sl, dl = pl.ds(0, ROW), pl.ds(SZ, ROW)
        return sp, sl, dp, dl

    def inside(dx, dy):
        return (gx + dx >= 0) & (gx + dx < GX) & (gy + dy >= 0) & (gy + dy < GY)

    def halo_copy(k):
        dx, dy = DIRS[k]
        sp, sl, dp, dl = where(DIRS[k])
        dev = {}
        if dx:
            dev["gx"] = gx + dx
        if dy:
            dev["gy"] = gy + dy
        return send(
            pg_ref.at[sp, :, sl], pg3.at[dp, pl.ds(C, C), dl], halo_s.at[k], halo_r.at[k], dev
        )

    for k, (dx, dy) in enumerate(DIRS):
        _, _, dp, dl = where((dx, dy))

        @pl.when(jnp.logical_not(inside(-dx, -dy)))
        def _(dp=dp, dl=dl):
            pg3[dp, C : 2 * C, dl] = jnp.zeros((dp.size, C, dl.size), BF)

    row = lax.broadcasted_iota(jnp.int32, (PROW, SZ), 0)
    col = lax.broadcasted_iota(jnp.int32, (PROW, SZ), 1)
    pack[:, 0:SZ] = jnp.where(row == col * SZ + SZ - 1, 1.0, 0.0).astype(BF)
    pack[:, SZ:] = jnp.where(row == col * SZ, 1.0, 0.0).astype(BF)
    row = lax.broadcasted_iota(jnp.int32, (SZ, PROW), 0)
    col = lax.broadcasted_iota(jnp.int32, (SZ, PROW), 1)
    spread[0] = jnp.where(col == row * SZ, 1.0, 0.0).astype(BF)
    spread[1] = jnp.where(col == row * SZ + SZ - 1, 1.0, 0.0).astype(BF)

    pl.semaphore_wait(barrier, GX + GY + GZ - 3 + 4)

    for k in range(1, GZ):
        send(wp_ref, az.at[k - 1], az_s.at[k - 1], az_r.at[k - 1], {"gz": lax.rem(gz + k, GZ)}).start()
    for k, (dx, dy) in enumerate(DIRS):

        @pl.when(inside(dx, dy))
        def _(k=k):
            halo_copy(k).start()

    xhi = jnp.zeros((C, SZ), F32)
    xlo = jnp.zeros((C, SZ), F32)
    for i in range(SX):
        t = dot(x_ref[i], pack[SZ : SZ + ROW, :], NN)
        xhi = xhi + pltpu.roll(t[:, :SZ], 10 * (i + 1), 1)
        xlo = xlo + pltpu.roll(t[:, SZ:], 10 * (i + 1), 1)
    for a in range(3):
        xroll[0, a * C : (a + 1) * C, :] = pltpu.roll(xhi, (-10 * (a - 1)) % SZ, 1).astype(BF)
        xroll[1, a * C : (a + 1) * C, :] = pltpu.roll(xlo, (-10 * (a - 1)) % SZ, 1).astype(BF)
    gacc[...] = jnp.zeros(gacc.shape, F32)
    acc[...] = jnp.zeros(acc.shape, F32)

    for k, (dx, dy) in enumerate(DIRS):

        @pl.when(inside(-dx, -dy))
        def _(k=k):
            halo_copy(k).wait_recv()

    xface[...] = jnp.zeros(xface.shape, F32)

    def pack_faces(px, carry):
        t = dot(pg3[px, C : 2 * C, :], pack[...], NN)
        xface[0] += pltpu.roll(t[:, :SZ], 10 * px, 1)
        xface[1] += pltpu.roll(t[:, SZ:], 10 * px, 1)
        return carry

    lax.fori_loop(0, SX + 2, pack_faces, 0)
    zsend[...] = xface[...].astype(BF)

    def z_copy(face):
        return send(
            zsend.at[face], zrecv.at[face], z_s.at[face], z_r.at[face], {"gz": gz + (1 - 2 * face)}
        )

    has = ((gz < GZ - 1), (gz > 0))
    for face in range(2):

        @pl.when(has[face])
        def _(face=face):
            z_copy(face).start()

        @pl.when(jnp.logical_not(has[1 - face]))
        def _(face=face):
            zrecv[face] = jnp.zeros((C, SZ), BF)

    for k in range(1, GZ):
        send(wp_ref, az.at[k - 1], az_s.at[k - 1], az_r.at[k - 1], {"gz": lax.rem(gz + k, GZ)}).wait()
    w = wp_ref[...].astype(F32)
    for k in range(GZ - 1):
        w = w + az[k].astype(F32)
    ax[gx, gy] = w.astype(BF)

    def ay_copy(k):
        return send(
            ax.at[gx, gy], ax.at[gx, gy], ay_s.at[k - 1], ay_r.at[k - 1], {"gy": lax.rem(gy + k, GY)}
        )

    for k in range(1, GY):
        ay_copy(k).start()

    lane = lanes((C, SZ))

    def shift(px, carry):
        for j in range(SY + 2):
            t = pg3[px, C : 2 * C, j * SZ : (j + 1) * SZ].astype(F32)
            up = jnp.where(lane == 0, 0.0, pltpu.roll(t, 1, 1))
            down = jnp.where(lane == SZ - 1, 0.0, pltpu.roll(t, SZ - 1, 1))
            pg3[px, 2 * C :, j * SZ : (j + 1) * SZ] = up.astype(BF)
            pg3[px, 0:C, j * SZ : (j + 1) * SZ] = down.astype(BF)
        return carry

    lax.fori_loop(0, SX + 2, shift, 0)

    def wgrad(px, carry):
        xs = x12[pl.ds(pl.multiple_of(px * C, C), 3 * C), :]
        for b in range(3):
            win = pg3[px, :, (2 - b) * SZ : (2 - b) * SZ + ROW]
            gacc[b, :, 0 : 3 * C] += dot(win, xs, NT)
        return carry

    lax.fori_loop(0, SX // 2 + 1, wgrad, 0)

    for k in range(1, GY):
        ay_copy(k).wait()

    def ax_copy(k):
        return send(ax.at[gx], ax.at[gx], ax_s.at[k - 1], ax_r.at[k - 1], {"gx": lax.rem(gx + k, GX)})

    for k in range(1, GX):
        ax_copy(k).start()

    lax.fori_loop(SX // 2 + 1, SX + 2, wgrad, 0)

    for face in range(2):

        @pl.when(has[1 - face])
        def _(face=face):
            z_copy(face).wait_recv()

    for face in range(2):
        c = 2 - 2 * face
        z = zrecv[face].astype(F32)
        for b in range(3):
            zb = pltpu.roll(z, (b - 1) % SZ, 1).astype(BF)
            gacc[b, c * C : (c + 1) * C, 0 : 3 * C] += dot(zb, xroll[1 - face], NT)

    half = lanes((C // 2, SZ)) < C
    dfull[27] = jnp.zeros((C // 2, SZ), F32)
    for b in range(3):
        for c in range(3):
            even, odd = c * C, c * C + C // 2
            e0, o0 = gacc[b, even:odd, 0:SZ], gacc[b, odd : odd + C // 2, 0:SZ]
            e1, o1 = gacc[b, even:odd, SZ:], gacc[b, odd : odd + C // 2, SZ:]
            t = b * 3 + c
            dfull[t] = jnp.where(half, e0, pltpu.roll(o0, C, 1))
            dfull[9 + t] = jnp.where(half, pltpu.roll(e0, C, 1), o0)
            dfull[18 + t] = jnp.where(half, e1, pltpu.roll(o1, C, 1))
    for u in range(14):
        for g in range(GX):
            pair = jnp.concatenate([dfull[2 * u, g * 8 : g * 8 + 8], dfull[2 * u + 1, g * 8 : g * 8 + 8]], 0)
            sx[g, u * 16 : (u + 1) * 16, :] = pair.astype(BF)

    def rx_copy(k):
        peer = lax.rem(gx + k, GX)
        return send(sx.at[peer], rx.at[k - 1], rx_s.at[k - 1], rx_r.at[k - 1], {"gx": peer})

    for k in range(1, GX):
        rx_copy(k).start()

    for k in range(1, GX):
        ax_copy(k).wait()
    for i in range(GX):
        for j in range(GY):
            r = (i * GY + j) * 32
            wf[r : r + 32, :] = ax[i, j].astype(F32)
    for b in range(3):
        wk[b, 3 * C :, :] = jnp.zeros((C, 2 * SZ), F32)
        for c in range(3):
            a0 = wf[pl.ds(b * 3 + c, 32, stride=32), :]
            a1 = wf[pl.ds(9 + b * 3 + c, 32, stride=32), :]
            a2 = wf[pl.ds(18 + b * 3 + c, 32, stride=32), :]
            r0, r1, r2 = (pltpu.roll(v, C, 1) for v in (a0, a1, a2))
            wk[b, c * C : c * C + 32, 0:SZ] = jnp.where(half, a0, r1)
            wk[b, c * C : c * C + 32, SZ:] = a2
            wk[b, c * C + 32 : c * C + 64, 0:SZ] = jnp.where(half, r0, a1)
            wk[b, c * C + 32 : c * C + 64, SZ:] = r2
        for m in range(2):
            for n in range(2):
                t = wk[b, n * SZ : (n + 1) * SZ, m * SZ : (m + 1) * SZ]
                wl[b, m * SZ : (m + 1) * SZ, n * SZ : (n + 1) * SZ] = t.T.astype(BF)

    xface[...] = zrecv[...].astype(F32)

    def patch(px, carry):
        back = lax.rem(SZ - 10 * px, SZ)
        for face in range(2):
            c = 2 - 2 * face
            t = pltpu.roll(xface[face], back, 1).astype(BF)
            put = dot(t, spread[face], NN)
            old = pg3[px, c * C : (c + 1) * C, :].astype(F32)
            pg3[px, c * C : (c + 1) * C, :] = (old + put).astype(BF)
        return carry

    lax.fori_loop(0, SX + 2, patch, 0)

    def dgrad(px, carry):
        at = pl.ds(pl.multiple_of(px * C, C), 3 * C)
        for n in range(4):
            y = None
            for b in range(3):
                lo = (2 - b) * SZ + n * 256
                d = dot(wl[b, 0 : 3 * C, 0 : 3 * C], pg3[px, :, lo : lo + 256], NN)
                y = d if y is None else y + d
            acc[at, n * 256 : (n + 1) * 256] += y
        return carry

    lax.fori_loop(0, 4, dgrad, 0)

    for k in range(1, GX):
        rx_copy(k).wait()
    mine = pl.ds(pl.multiple_of(gx * 8, 8), 8)
    for u in range(14):
        v = jnp.concatenate([dfull[2 * u, mine, :], dfull[2 * u + 1, mine, :]], 0)
        for k in range(GX - 1):
            v = v + rx[k, u * 16 : (u + 1) * 16, :].astype(F32)
        ef[u * 16 : (u + 1) * 16, :] = v
    ef[224:, :] = jnp.zeros((32, SZ), F32)
    for g in range(GY):
        v = ef[pl.ds(g, 32, stride=8), :]
        ff[g] = v
        sy[g] = v.astype(BF)

    def ry_copy(k):
        peer = lax.rem(gy + k, GY)
        return send(sy.at[peer], ry.at[k - 1], ry_s.at[k - 1], ry_r.at[k - 1], {"gy": peer})

    for k in range(1, GY):
        ry_copy(k).start()

    lax.fori_loop(4, 7, dgrad, 0)

    for k in range(1, GY):
        ry_copy(k).wait()
    v = ff[gy]
    for k in range(GY - 1):
        v = v + ry[k].astype(F32)
    v = jnp.concatenate([v, jnp.zeros((96, SZ), F32)], 0)
    szf[...] = v.T

    def rz_copy(k):
        peer = lax.rem(gz + k, GZ)
        return send(
            szf.at[pl.ds(pl.multiple_of(peer * 16, 16), 16), :], rz.at[k - 1], rz_s.at[k - 1], rz_r.at[k - 1], {"gz": peer}
        )

    for k in range(1, GZ):
        rz_copy(k).start()

    lax.fori_loop(7, SX + 2, dgrad, 0)
    for i in range(SX):
        out_ref[i] = acc[(i + 2) * C : (i + 3) * C, :].astype(BF)

    for k in range(1, GZ):
        rz_copy(k).wait()
    v = szf[pl.ds(pl.multiple_of(gz * 16, 16), 16), :]
    for k in range(GZ - 1):
        v = v + rz[k]
    wg_ref[...] = v

    for k, (dx, dy) in enumerate(DIRS):

        @pl.when(inside(dx, dy))
        def _(k=k):
            halo_copy(k).wait_send()

    for face in range(2):

        @pl.when(has[face])
        def _(face=face):
            z_copy(face).wait_send()


def call(pg, x, wp):
    vmem = pl.BlockSpec(memory_space=pltpu.VMEM)
    dma = pltpu.SemaphoreType.DMA
    v = pltpu.VMEM
    return pl.pallas_call(
        kernel,
        out_shape=(
            jax.ShapeDtypeStruct((SX, C, ROW), BF),
            jax.ShapeDtypeStruct((16, SZ), F32),
        ),
        in_specs=[vmem] * 3,
        out_specs=(vmem, vmem),
        scratch_shapes=[
            v((SX + 2, 3 * C, PROW), BF),
            v(((SX + 4) * C, ROW), BF),
            v((PROW, 2 * SZ), BF),
            v((2, SZ, PROW), BF),
            v((3, 3 * C, 2 * SZ), F32),
            v((28, C // 2, SZ), F32),
            v(((SX + 4) * C, ROW), F32),
            v((2, C, SZ), BF),
            v((2, C, SZ), BF),
            v((2, C, SZ), F32),
            v((2, 3 * C, SZ), BF),
            v((GZ - 1, 32, SZ), BF),
            v((GX, GY, 32, SZ), BF),
            v((1024, SZ), F32),
            v((3, 2 * SZ, 2 * SZ), F32),
            v((3, 2 * SZ, 2 * SZ), BF),
            v((GX, 224, SZ), BF),
            v((GX - 1, 224, SZ), BF),
            v((256, SZ), F32),
            v((GY, 32, SZ), F32),
            v((GY, 32, SZ), BF),
            v((GY - 1, 32, SZ), BF),
            v((SZ, SZ), F32),
            v((GZ - 1, 16, SZ), F32),
            dma((8,)), dma((8,)), dma((2,)), dma((2,)),
            dma((GZ - 1,)), dma((GZ - 1,)), dma((GY - 1,)), dma((GY - 1,)), dma((GX - 1,)), dma((GX - 1,)),
            dma((GX - 1,)), dma((GX - 1,)), dma((GY - 1,)), dma((GY - 1,)), dma((GZ - 1,)), dma((GZ - 1,)),
        ],
        compiler_params=pltpu.CompilerParams(
            collective_id=0, has_side_effects=True, vmem_limit_bytes=56 * 1024 * 1024
        ),
    )(pg, x, wp)


def local(activations, preact, upstream, master, first_moment, second_moment):
    pre_grad = jnp.where(preact > 0, upstream, jnp.zeros_like(upstream))
    pg = jnp.transpose(pre_grad.reshape(C // 2, 2, SX, SY, SZ), (2, 1, 0, 3, 4)).reshape(SX, C, ROW)
    x = jnp.transpose(activations, (1, 0, 2, 3)).reshape(SX, C, ROW)
    w = jnp.pad(master.astype(BF).reshape(16, 27).T, ((0, 5), (0, 0)))
    own = lax.broadcasted_iota(jnp.int32, (32, SZ), 1) // 16 == lax.axis_index("gz")
    wp = jnp.where(own, jnp.tile(w, (1, 8)), jnp.zeros((), BF))
    out, wg = call(pg, x, wp)
    grad_input = jnp.transpose(out.reshape(SX, C, SY, SZ), (1, 0, 2, 3))
    voxels = SX * SY * SZ * GX * GY * GZ
    weight_grad = wg[:, :27].reshape(-1) / math.sqrt(voxels)
    new_first = 0.9 * first_moment + 0.1 * weight_grad
    new_second = 0.999 * second_moment + 0.001 * weight_grad * weight_grad
    corr_first = 1.0 - (0.9**10) ** 10
    corr_second = 1.0 - (0.999**10) ** 10
    update = new_first / corr_first / (jnp.sqrt(new_second / corr_second) + 1e-08) + 0.01 * master
    new_master = master - 0.05 * update
    return (grad_input, weight_grad, new_master, new_first, new_second)


def solution(mesh):
    vol = P(None, "gx", "gy", "gz")
    par = P(("gx", "gy", "gz"))
    return jax.shard_map(
        local,
        mesh=mesh,
        in_specs=(vol, vol, vol, par, par, par),
        out_specs=(vol, par, par, par, par),
        check_vma=False,
    )
```

time: 662 us -> 57.4 us (0.09)
  waiting for transfers between devices: 512 us -> 0 us
  local copies, waits for them, and re-layouts: 78.7 us -> 9.07 us
  Pallas kernels: 0 us -> 46 us
  matrix products: 23.4 us -> 0 us
  starting transfers between devices: 17 us -> 0 us
  between operations: 14.5 us -> 0.77 us
  other arithmetic: 15 us -> 1.37 us
    unnamed x4 -> x0, waiting for transfers between devices: 497 us -> none
    pallas_call x0 -> x1, Pallas kernels: none -> 46 us  [call(): pl.pallas_call(kernel, out_shape=(jax.ShapeDtypeStruct((SX, C, ROW), BF),...]
    reshape x2 -> x5, local copies, waits for them, and re-layouts: 30.5 us -> 4.69 us  [the longest x2 3.07 us: local(): x = jnp.transpose(activations, (1, 0, 2, 3)).reshape(SX, C, ROW)]
    ppermute x6 -> x0, starting transfers between devices: 16.9 us -> none  [the longest x3 12.4 us: padded_2(): lax.ppermute(lax.slice_in_dim(block, block.shape[dim] - width, None, axis...]
    ppermute x6 -> x0, waiting for transfers between devices: 14.3 us -> none  [the longest x3 8.62 us: padded_2(): lax.ppermute(lax.slice_in_dim(block, 0, width, axis=dim), axis, backward)]
    slice x4 -> x0, local copies, waits for them, and re-layouts: 13.9 us -> none  [the longest x2 7.89 us: padded_2(): lax.slice_in_dim(block, block.shape[dim] - width, None, axis=dim)]
    dot_general x27 -> x0, matrix products: 13.7 us -> none  [local(): lax.dot_general(pre_grad, window, (((1, 2, 3), (1, 2, 3)), ((), ())), pre...]
    conv_general_dilated x3 -> x0, local copies, waits for them, and re-layouts: 11 us -> none  [local(): lax.conv_general_dilated(padded_grad[None], flipped, (1, 1, 1), 'VALID',...]
  transfers between devices with their start and end apart: 8 -> 0, of which waited for: 7 -> 0; matrix products, arithmetic and copies ran while one was open for 4% -> 0% of each run, Pallas kernels for 0% -> 0%
where the time goes in v1:
time: 57.4 us; the launch traced here: 57.2 us
  Pallas kernels  46 us (80%)
  local copies, waits for them, and re-layouts  9.07 us (16%)
  other arithmetic  1.37 us (2%)
  between operations  0.77 us (1%)
    pallas_call x1, Pallas kernels, call(): pl.pallas_call(kernel, out_shape=(jax.ShapeDtypeStruct((SX, C, ROW), BF),...  46 us
    reshape x2, local copies, waits for them, and re-layouts, local(): x = jnp.transpose(activations, (1, 0, 2, 3)).reshape(SX, C, ROW)  3.07 us
    unnamed x15, local copies, waits for them, and re-layouts  2.77 us
    reshape x1, local copies, waits for them, and re-layouts, local(): jnp.transpose(pre_grad.reshape(C // 2, 2, SX, SY, SZ), (2, 1, 0, 3, 4))  1.27 us
    transpose x1, local copies, waits for them, and re-layouts, local(): grad_input = jnp.transpose(out.reshape(SX, C, SY, SZ), (1, 0, 2, 3))  1.27 us

profile of v1, /device:TPU:1, one launch (start us, length us, event | category | flops | bytes accessed | tf_op | source)
XLA Modules:
  0.0 57.2 jit_solution(14062571773088197909)
XLA Ops:
  0.6 0.0 copy-start.3
  0.7 0.7 %copy-done.3 = f32[432]{0:T(512)S(1)} copy-done((f32[432]{0:T(512)S(1)}, f32[432]{0:T(512)}, u32[]{:S(2)}) %copy-start.3) | copy-done | bytes 1752
  1.3 0.1 reshape.39
  1.4 0.1 copy.16
  1.5 0.6 %fusion.wp_ref = bf16[32,128]{1,0:T(8,128)(2,1)} fusion(bf16[32,128]{1,0:T(8,128)(2,1)S(1)} %copy.16, s32[]{:T(128)S(6)} %axis_index.12, s32[128]{0:T(128)S(1)} %get-tuple-element.15, s32[128]{0:T(128)S(1)} %get-tuple-element.16, pred[128]{0:T(512)(128)(4,1)S(1)} %compare_and_fusion), kind=kLoop, calls=%fused_computation.4 | loop fusion | flops 12288 | bytes 17540 | tf_op jit(solution)/shard_map/jit(_where)/select_n | solution.py:420
  2.1 1.5 %reshape.41 = bf16[8,64,1024]{2,0,1:T(8,128)(2,1)S(1)} reshape(bf16[8,64,8,128]{3,2,0,1:T(8,128)(2,1)} %bitcast.26) | data formatting | bytes 2097152 | tf_op jit(solution)/shard_map/reshape | solution.py:417
  3.7 0.0 copy-start
  3.7 0.0 copy-start.1
  3.7 1.6 %copy.18.x_ref = bf16[8,64,1024]{2,1,0:T(8,128)(2,1)} copy(bf16[8,64,1024]{2,0,1:T(8,128)(2,1)S(1)} %reshape.41) | data formatting | bytes 2097152 | tf_op jit(solution)/shard_map/reshape | solution.py:417
  5.2 0.0 copy-done
  5.2 0.0 copy-done.1
  5.3 0.1 compare_select_fusion
  5.4 0.3 copy.22
  5.6 1.3 %reshape.37.pg_ref = bf16[8,64,1024]{2,1,0:T(8,128)(2,1)} reshape(bf16[8,2,32,8,128]{4,3,2,1,0:T(8,128)(2,1)S(1)} %bitcast.24) | data formatting | bytes 2097152 | tf_op jit(solution)/shard_map/reshape | solution.py:416
  6.9 46.0 %shard_map.101 = (bf16[8,64,1024]{2,1,0:T(8,128)(2,1)}, f32[16,128]{1,0:T(8,128)}) custom-call(bf16[8,64,1024]{2,1,0:T(8,128)(2,1)} %reshape.37.pg_ref, bf16[8,64,1024]{2,1,0:T(8,128)(2,1)} %copy.18.x_ref, bf16[32,128]{1,0:T(8,128)(2,1)} %fusion.wp_ref), custom_call_target="tpu_custom_call" | custom-call | tf_op jit(solution)/shard_map/pallas_call | solution.py:371
  52.9 1.5 %copy.19 = bf16[64,8,8,128]{3,2,1,0:T(8,128)(2,1)S(1)} copy(bf16[64,8,8,128]{3,1,2,0:T(8,128)(2,1)} %bitcast.27) | data formatting | bytes 2097152
  54.4 0.0 copy-start.4
  54.4 1.3 %copy_bitcast_fusion = bf16[64,8,8,128]{3,2,1,0:T(8,128)(2,1)} fusion(bf16[8,64,8,128]{3,2,1,0:T(8,128)(2,1)S(1)} %bitcast.25), kind=kLoop, calls=%fused_computation.1 | loop fusion | bytes 2097152 | tf_op jit(solution)/shard_map/transpose | solution.py:422
  55.7 0.0 copy-done.4
  55.7 0.1 mul.54
  55.8 0.1 div.36
  55.9 0.0 copy-start.2
  55.9 0.0 copy-start.5
  55.9 0.0 copy-start.6
  55.9 0.1 mul.49
  56.0 0.5 copy-done.2
  56.5 0.1 copy-done.5
  56.6 0.0 copy-done.6
  56.6 0.6 %multiply_subtract_fusion = (f32[432]{0:T(512)}, f32[432]{0:T(512)}, f32[432]{0:T(512)}) fusion(f32[432]{0:T(512)S(1)} %copy-done.3, f32[432]{0:T(512)S(1)} %mul.49, f32[432]{0:T(512)S(1)} %copy-done.5, f32[432]{0:T(512)S(1)} %mul.54, f32[432]{0:T(512)S(1)} %div.36, f32[432]{0:T(512)S(1)} %copy-done.6), kind=kLoop, calls=%fused_computation.8 | loop fusion | flops 5616 | bytes 15552 | tf_op jit(solution)/shard_map/sub | solution.py:430
  (6 shorter events, 0.0 us)
Async XLA Ops:
  0.6 0.7 %copy-start.3 = (f32[432]{0:T(512)S(1)}, f32[432]{0:T(512)}, u32[]{:S(2)}) copy-start(f32[432]{0:T(512)} %param.9) | copy-start | bytes 5188
  3.7 1.6 %copy-start = (bf16[64,8,8,128]{3,2,1,0:T(8,128)(2,1)S(1)}, bf16[64,8,8,128]{3,2,1,0:T(8,128)(2,1)}, u32[]{:S(2)}) copy-start(bf16[64,8,8,128]{3,2,1,0:T(8,128)(2,1)} %param.8) | copy-start | bytes 3145732
  3.7 1.6 %copy-start.1 = (bf16[64,8,8,128]{3,2,1,0:T(8,128)(2,1)S(1)}, bf16[64,8,8,128]{3,2,1,0:T(8,128)(2,1)}, u32[]{:S(2)}) copy-start(bf16[64,8,8,128]{3,2,1,0:T(8,128)(2,1)} %param.7) | copy-start | bytes 3145732
  54.4 1.3 %copy-start.4 = (f32[16,128]{1,0:T(8,128)S(1)}, f32[16,128]{1,0:T(8,128)}, u32[]{:S(2)}) copy-start(f32[16,128]{1,0:T(8,128)} %get-tuple-element.8) | copy-start | bytes 24580
  55.9 0.6 %copy-start.2 = (f32[432]{0:T(512)}, f32[432]{0:T(512)S(1)}, u32[]{:S(2)}) copy-start(f32[432]{0:T(512)S(1)} %div.36) | copy-start | bytes 5188
  55.9 0.7 %copy-start.5 = (f32[432]{0:T(512)S(1)}, f32[432]{0:T(512)}, u32[]{:S(2)}) copy-start(f32[432]{0:T(512)} %param.10) | copy-start | bytes 5188
  55.9 0.7 %copy-start.6 = (f32[432]{0:T(512)S(1)}, f32[432]{0:T(512)}, u32[]{:S(2)}) copy-start(f32[432]{0:T(512)} %param.11) | copy-start | bytes 5188

commit v2 on v1

--- a/solution.py
+++ b/solution.py
@@ -9,6 +9,8 @@
 from jax.sharding import PartitionSpec as P
 
 MESH = pl.DeviceIdType.MESH
+TRACE = False
+_scope = [None]
 BF, F32 = jnp.bfloat16, jnp.float32
 GX, GY, GZ = 4, 8, 8
 C = 64
@@ -24,17 +26,28 @@
     return lax.dot_general(a, b, dims, preferred_element_type=F32)
 
 
+def mark(name):
+    if not TRACE:
+        return
+    if _scope[0] is not None:
+        _scope[0].__exit__(None, None, None)
+        _scope[0] = None
+    if name:
+        _scope[0] = jax.named_scope(name)
+        _scope[0].__enter__()
+
+
 def lanes(shape):
     return lax.broadcasted_iota(jnp.int32, shape, 1)
 
 
 def kernel(
     pg_ref, x_ref, wp_ref, out_ref, wg_ref,
-    pg3, x12, pack, spread, gacc, dfull, acc,
-    zsend, zrecv, xface, xroll,
+    pg3, x3, pack, spread, gacc, dfull, acc,
+    zsend, zrecv, xsend, xrecv,
     az, ax, wf, wk, wl,
     sx, rx, ef, ff, sy, ry, szf, rz,
-    halo_s, halo_r, z_s, z_r, az_s, az_r, ay_s, ay_r, ax_s, ax_r,
+    halo_s, halo_r, z_s, z_r, xz_s, xz_r, az_s, az_r, ay_s, ay_r, ax_s, ax_r,
     rx_s, rx_r, ry_s, ry_r, rz_s, rz_r,
 ):
     gx, gy, gz = lax.axis_index("gx"), lax.axis_index("gy"), lax.axis_index("gz")
@@ -44,6 +57,7 @@
             src_ref=src, dst_ref=dst, send_sem=ss, recv_sem=rs, device_id=dev, device_id_type=MESH
         )
 
+    mark("barsig")
     barrier = pltpu.get_barrier_semaphore()
     for k in range(1, GX):
         pl.semaphore_signal(barrier, inc=1, device_id={"gx": lax.rem(gx + k, GX)}, device_id_type=MESH)
@@ -59,11 +73,8 @@
             device_id_type=MESH,
         )
 
+    mark("prep")
     pg3[1 : SX + 1, C : 2 * C, SZ : SZ + ROW] = pg_ref[...]
-    x12[0 : 2 * C, :] = jnp.zeros((2 * C, ROW), BF)
-    x12[(SX + 2) * C :, :] = jnp.zeros((2 * C, ROW), BF)
-    for i in range(SX):
-        x12[(i + 2) * C : (i + 3) * C, :] = x_ref[i]
 
     def where(d):
         sxd, syd = d
@@ -107,56 +118,103 @@
     col = lax.broadcasted_iota(jnp.int32, (PROW, SZ), 1)
     pack[:, 0:SZ] = jnp.where(row == col * SZ + SZ - 1, 1.0, 0.0).astype(BF)
     pack[:, SZ:] = jnp.where(row == col * SZ, 1.0, 0.0).astype(BF)
-    row = lax.broadcasted_iota(jnp.int32, (SZ, PROW), 0)
-    col = lax.broadcasted_iota(jnp.int32, (SZ, PROW), 1)
-    spread[0] = jnp.where(col == row * SZ, 1.0, 0.0).astype(BF)
-    spread[1] = jnp.where(col == row * SZ + SZ - 1, 1.0, 0.0).astype(BF)
-
+
+    has = ((gz < GZ - 1), (gz > 0))
+
+    def faces(planes, first):
+        n = planes.shape[0]
+        t = dot(planes.reshape(n * C, planes.shape[2]), pack[0 : planes.shape[2], :], NN)
+        high = jnp.zeros((C, SZ), F32)
+        low = jnp.zeros((C, SZ), F32)
+        for i in range(n):
+            high = high + pltpu.roll(t[i * C : (i + 1) * C, :SZ], 10 * i, 1)
+            low = low + pltpu.roll(t[i * C : (i + 1) * C, SZ:], 10 * i, 1)
+        return high, low
+
+    def x_copy(face):
+        return send(
+            xsend.at[face], xrecv.at[face], xz_s.at[face], xz_r.at[face], {"gz": gz + (1 - 2 * face)}
+        )
+
+    def z_copy(face):
+        return send(
+            zsend.at[face], zrecv.at[face], z_s.at[face], z_r.at[face], {"gz": gz + (1 - 2 * face)}
+        )
+
+    mark("xfaces")
+    high, low = faces(x_ref[...], 0)
+    xsend[0] = high.astype(BF)
+    xsend[1] = low.astype(BF)
+
+    mark("barwait")
     pl.semaphore_wait(barrier, GX + GY + GZ - 3 + 4)
 
-    for k in range(1, GZ):
-        send(wp_ref, az.at[k - 1], az_s.at[k - 1], az_r.at[k - 1], {"gz": lax.rem(gz + k, GZ)}).start()
+    mark("start")
     for k, (dx, dy) in enumerate(DIRS):
 
         @pl.when(inside(dx, dy))
         def _(k=k):
             halo_copy(k).start()
 
-    xhi = jnp.zeros((C, SZ), F32)
-    xlo = jnp.zeros((C, SZ), F32)
-    for i in range(SX):
-        t = dot(x_ref[i], pack[SZ : SZ + ROW, :], NN)
-        xhi = xhi + pltpu.roll(t[:, :SZ], 10 * (i + 1), 1)
-        xlo = xlo + pltpu.roll(t[:, SZ:], 10 * (i + 1), 1)
-    for a in range(3):
-        xroll[0, a * C : (a + 1) * C, :] = pltpu.roll(xhi, (-10 * (a - 1)) % SZ, 1).astype(BF)
-        xroll[1, a * C : (a + 1) * C, :] = pltpu.roll(xlo, (-10 * (a - 1)) % SZ, 1).astype(BF)
+    for face in range(2):
+
+        @pl.when(has[face])
+        def _(face=face):
+            x_copy(face).start()
+
+        @pl.when(jnp.logical_not(has[1 - face]))
+        def _(face=face):
+            xrecv[face] = jnp.zeros((C, SZ), BF)
+
+    for k in range(1, GZ):
+        send(wp_ref, az.at[k - 1], az_s.at[k - 1], az_r.at[k - 1], {"gz": lax.rem(gz + k, GZ)}).start()
+
+    mark("xshift")
+    lane = lanes((C, SZ))
     gacc[...] = jnp.zeros(gacc.shape, F32)
+
+    def xshift(i, carry):
+        x3[i, C : 2 * C, :] = x_ref[i]
+        for j in range(SY):
+            t = x_ref[i, :, j * SZ : (j + 1) * SZ].astype(F32)
+            up = jnp.where(lane == 0, 0.0, pltpu.roll(t, 1, 1))
+            down = jnp.where(lane == SZ - 1, 0.0, pltpu.roll(t, SZ - 1, 1))
+            x3[i, 0:C, j * SZ : (j + 1) * SZ] = up.astype(BF)
+            x3[i, 2 * C :, j * SZ : (j + 1) * SZ] = down.astype(BF)
+        return carry
+
+    lax.fori_loop(0, SX, xshift, 0)
+
+    CUT = ((256, 0, 896), (128, 0, 1024), (128, 128, 896))
+
+    def wdot(plane, n, q, b, lo):
+        ps, xo, size = CUT[b]
+        win = pg3[pl.ds(plane, n), C : 2 * C, ps : ps + size].reshape(n * C, size)
+        gacc[b, lo * C : (lo + n) * C, 0 : 3 * C] += dot(win, x3[q, :, xo : xo + size], NT)
+
+    def wgrad(q, carry):
+        for b in range(3):
+            wdot(q, 3, q, b, 0)
+        return carry
+
+    mark("wgrad")
+    lax.fori_loop(1, SX - 1, wgrad, 0)
+    for b in range(3):
+        wdot(1, 2, 0, b, 1)
+        wdot(SX - 1, 2, SX - 1, b, 0)
     acc[...] = jnp.zeros(acc.shape, F32)
 
+    mark("halowait")
     for k, (dx, dy) in enumerate(DIRS):
 
         @pl.when(inside(-dx, -dy))
         def _(k=k):
             halo_copy(k).wait_recv()
 
-    xface[...] = jnp.zeros(xface.shape, F32)
-
-    def pack_faces(px, carry):
-        t = dot(pg3[px, C : 2 * C, :], pack[...], NN)
-        xface[0] += pltpu.roll(t[:, :SZ], 10 * px, 1)
-        xface[1] += pltpu.roll(t[:, SZ:], 10 * px, 1)
-        return carry
-
-    lax.fori_loop(0, SX + 2, pack_faces, 0)
-    zsend[...] = xface[...].astype(BF)
-
-    def z_copy(face):
-        return send(
-            zsend.at[face], zrecv.at[face], z_s.at[face], z_r.at[face], {"gz": gz + (1 - 2 * face)}
-        )
-
-    has = ((gz < GZ - 1), (gz > 0))
+    mark("pgfaces")
+    zhigh, zlow = faces(pg3[:, C : 2 * C, :], 0)
+    zsend[0] = zhigh.astype(BF)
+    zsend[1] = zlow.astype(BF)
     for face in range(2):
 
         @pl.when(has[face])
@@ -167,6 +225,7 @@
         def _(face=face):
             zrecv[face] = jnp.zeros((C, SZ), BF)
 
+    mark("azwait")
     for k in range(1, GZ):
         send(wp_ref, az.at[k - 1], az_s.at[k - 1], az_r.at[k - 1], {"gz": lax.rem(gz + k, GZ)}).wait()
     w = wp_ref[...].astype(F32)
@@ -182,7 +241,58 @@
     for k in range(1, GY):
         ay_copy(k).start()
 
-    lane = lanes((C, SZ))
+    mark("wedge")
+    for b in range(3):
+        wdot(0, 1, 0, b, 0)
+        wdot(SX + 1, 1, SX - 1, b, 2)
+    for b, ps, xo in ((2, 0, 0), (0, PROW - SZ, ROW - SZ)):
+        y = None
+        for q in range(0, SX, 2):
+            left = [pg3[v : v + 3, C : 2 * C, ps : ps + SZ].reshape(3 * C, SZ) for v in (q, q + 1)]
+            right = [x3[v, :, xo : xo + SZ] for v in (q, q + 1)]
+            d = dot(jnp.concatenate(left, 1), jnp.concatenate(right, 1), NT)
+            y = d if y is None else y + d
+        gacc[b, :, 0 : 3 * C] += y
+
+    mark("xzwait")
+    for face in range(2):
+
+        @pl.when(has[1 - face])
+        def _(face=face):
+            x_copy(face).wait_recv()
+
+    mark("zcorr")
+    for face, local in ((0, zlow), (1, zhigh)):
+        c = 2 * face
+        for b in range(3):
+            rows = [pltpu.roll(local, (-(10 * j + 2 - b)) % SZ, 1) for j in range(3)]
+            rows = jnp.concatenate(rows, 0).astype(BF)
+            gacc[b, :, c * C : (c + 1) * C] += dot(rows, xrecv[face], NT)
+
+    mark("dfull")
+    half = lanes((C // 2, SZ)) < C
+    dfull[27] = jnp.zeros((C // 2, SZ), F32)
+    for b in range(3):
+        for a in range(3):
+            even = (2 - a) * C
+            odd = even + C // 2
+            e0, o0 = gacc[b, even:odd, 0:SZ], gacc[b, odd : odd + C // 2, 0:SZ]
+            e1, o1 = gacc[b, even:odd, SZ:], gacc[b, odd : odd + C // 2, SZ:]
+            t = a * 9 + b * 3
+            dfull[t] = jnp.where(half, e0, pltpu.roll(o0, C, 1))
+            dfull[t + 1] = jnp.where(half, pltpu.roll(e0, C, 1), o0)
+            dfull[t + 2] = jnp.where(half, e1, pltpu.roll(o1, C, 1))
+    for u in range(14):
+        for g in range(GX):
+            pair = jnp.concatenate([dfull[2 * u, g * 8 : g * 8 + 8], dfull[2 * u + 1, g * 8 : g * 8 + 8]], 0)
+            sx[g, u * 16 : (u + 1) * 16, :] = pair.astype(BF)
+
+    def rx_copy(k):
+        peer = lax.rem(gx + k, GX)
+        return send(sx.at[peer], rx.at[k - 1], rx_s.at[k - 1], rx_r.at[k - 1], {"gx": peer})
+
+    for k in range(1, GX):
+        rx_copy(k).start()
 
     def shift(px, carry):
         for j in range(SY + 2):
@@ -193,17 +303,10 @@
             pg3[px, 0:C, j * SZ : (j + 1) * SZ] = down.astype(BF)
         return carry
 
-    lax.fori_loop(0, SX + 2, shift, 0)
-
-    def wgrad(px, carry):
-        xs = x12[pl.ds(pl.multiple_of(px * C, C), 3 * C), :]
-        for b in range(3):
-            win = pg3[px, :, (2 - b) * SZ : (2 - b) * SZ + ROW]
-            gacc[b, :, 0 : 3 * C] += dot(win, xs, NT)
-        return carry
-
-    lax.fori_loop(0, SX // 2 + 1, wgrad, 0)
-
+    mark("shift1")
+    lax.fori_loop(0, 5, shift, 0)
+
+    mark("aywait")
     for k in range(1, GY):
         ay_copy(k).wait()
 
@@ -213,46 +316,58 @@
     for k in range(1, GX):
         ax_copy(k).start()
 
-    lax.fori_loop(SX // 2 + 1, SX + 2, wgrad, 0)
-
+    mark("shift2")
+    lax.fori_loop(5, SX + 2, shift, 0)
+    row = lax.broadcasted_iota(jnp.int32, (SZ, PROW), 0)
+    col = lax.broadcasted_iota(jnp.int32, (SZ, PROW), 1)
+    spread[0] = jnp.where(col == row * SZ, 1.0, 0.0).astype(BF)
+    spread[1] = jnp.where(col == row * SZ + SZ - 1, 1.0, 0.0).astype(BF)
+
+    mark("zwait")
     for face in range(2):
 
         @pl.when(has[1 - face])
         def _(face=face):
             z_copy(face).wait_recv()
 
+    mark("patch")
     for face in range(2):
         c = 2 - 2 * face
         z = zrecv[face].astype(F32)
-        for b in range(3):
-            zb = pltpu.roll(z, (b - 1) % SZ, 1).astype(BF)
-            gacc[b, c * C : (c + 1) * C, 0 : 3 * C] += dot(zb, xroll[1 - face], NT)
-
-    half = lanes((C // 2, SZ)) < C
-    dfull[27] = jnp.zeros((C // 2, SZ), F32)
-    for b in range(3):
-        for c in range(3):
-            even, odd = c * C, c * C + C // 2
-            e0, o0 = gacc[b, even:odd, 0:SZ], gacc[b, odd : odd + C // 2, 0:SZ]
-            e1, o1 = gacc[b, even:odd, SZ:], gacc[b, odd : odd + C // 2, SZ:]
-            t = b * 3 + c
-            dfull[t] = jnp.where(half, e0, pltpu.roll(o0, C, 1))
-            dfull[9 + t] = jnp.where(half, pltpu.roll(e0, C, 1), o0)
-            dfull[18 + t] = jnp.where(half, e1, pltpu.roll(o1, C, 1))
+        rows = [pltpu.roll(z, (-10 * i) % SZ, 1) for i in range(SX + 2)]
+        rows = jnp.concatenate(rows, 0).astype(BF)
+        for n in range(5):
+            put = dot(rows, spread[face, :, n * 256 : (n + 1) * 256], NN).reshape(SX + 2, C, 256)
+            old = pg3[:, c * C : (c + 1) * C, n * 256 : (n + 1) * 256].astype(F32)
+            pg3[:, c * C : (c + 1) * C, n * 256 : (n + 1) * 256] = (old + put).astype(BF)
+
+    mark("rxwait")
+    for k in range(1, GX):
+        rx_copy(k).wait()
+    mark("rxsum")
+    mine = pl.ds(pl.multiple_of(gx * 8, 8), 8)
     for u in range(14):
-        for g in range(GX):
-            pair = jnp.concatenate([dfull[2 * u, g * 8 : g * 8 + 8], dfull[2 * u + 1, g * 8 : g * 8 + 8]], 0)
-            sx[g, u * 16 : (u + 1) * 16, :] = pair.astype(BF)
-
-    def rx_copy(k):
-        peer = lax.rem(gx + k, GX)
-        return send(sx.at[peer], rx.at[k - 1], rx_s.at[k - 1], rx_r.at[k - 1], {"gx": peer})
-
-    for k in range(1, GX):
-        rx_copy(k).start()
-
+        v = jnp.concatenate([dfull[2 * u, mine, :], dfull[2 * u + 1, mine, :]], 0)
+        for k in range(GX - 1):
+            v = v + rx[k, u * 16 : (u + 1) * 16, :].astype(F32)
+        ef[u * 16 : (u + 1) * 16, :] = v
+    ef[224:, :] = jnp.zeros((32, SZ), F32)
+    for g in range(GY):
+        v = ef[pl.ds(g, 32, stride=8), :]
+        ff[g] = v
+        sy[g] = v.astype(BF)
+
+    def ry_copy(k):
+        peer = lax.rem(gy + k, GY)
+        return send(sy.at[peer], ry.at[k - 1], ry_s.at[k - 1], ry_r.at[k - 1], {"gy": peer})
+
+    for k in range(1, GY):
+        ry_copy(k).start()
+
+    mark("axwait")
     for k in range(1, GX):
         ax_copy(k).wait()
+    mark("wk")
     for i in range(GX):
         for j in range(GY):
             r = (i * GY + j) * 32
@@ -273,20 +388,6 @@
                 t = wk[b, n * SZ : (n + 1) * SZ, m * SZ : (m + 1) * SZ]
                 wl[b, m * SZ : (m + 1) * SZ, n * SZ : (n + 1) * SZ] = t.T.astype(BF)
 
-    xface[...] = zrecv[...].astype(F32)
-
-    def patch(px, carry):
-        back = lax.rem(SZ - 10 * px, SZ)
-        for face in range(2):
-            c = 2 - 2 * face
-            t = pltpu.roll(xface[face], back, 1).astype(BF)
-            put = dot(t, spread[face], NN)
-            old = pg3[px, c * C : (c + 1) * C, :].astype(F32)
-            pg3[px, c * C : (c + 1) * C, :] = (old + put).astype(BF)
-        return carry
-
-    lax.fori_loop(0, SX + 2, patch, 0)
-
     def dgrad(px, carry):
         at = pl.ds(pl.multiple_of(px * C, C), 3 * C)
         for n in range(4):
@@ -298,33 +399,13 @@
             acc[at, n * 256 : (n + 1) * 256] += y
         return carry
 
+    mark("dgrad1")
     lax.fori_loop(0, 4, dgrad, 0)
 
-    for k in range(1, GX):
-        rx_copy(k).wait()
-    mine = pl.ds(pl.multiple_of(gx * 8, 8), 8)
-    for u in range(14):
-        v = jnp.concatenate([dfull[2 * u, mine, :], dfull[2 * u + 1, mine, :]], 0)
-        for k in range(GX - 1):
-            v = v + rx[k, u * 16 : (u + 1) * 16, :].astype(F32)
-        ef[u * 16 : (u + 1) * 16, :] = v
-    ef[224:, :] = jnp.zeros((32, SZ), F32)
-    for g in range(GY):
-        v = ef[pl.ds(g, 32, stride=8), :]
-        ff[g] = v
-        sy[g] = v.astype(BF)
-
-    def ry_copy(k):
-        peer = lax.rem(gy + k, GY)
-        return send(sy.at[peer], ry.at[k - 1], ry_s.at[k - 1], ry_r.at[k - 1], {"gy": peer})
-
-    for k in range(1, GY):
-        ry_copy(k).start()
-
-    lax.fori_loop(4, 7, dgrad, 0)
-
+    mark("rywait")
     for k in range(1, GY):
         ry_copy(k).wait()
+    mark("rysum")
     v = ff[gy]
     for k in range(GY - 1):
         v = v + ry[k].astype(F32)
@@ -340,12 +421,15 @@
     for k in range(1, GZ):
         rz_copy(k).start()
 
-    lax.fori_loop(7, SX + 2, dgrad, 0)
+    mark("dgrad2")
+    lax.fori_loop(4, SX + 2, dgrad, 0)
     for i in range(SX):
         out_ref[i] = acc[(i + 2) * C : (i + 3) * C, :].astype(BF)
 
+    mark("rzwait")
     for k in range(1, GZ):
         rz_copy(k).wait()
+    mark("end")
     v = szf[pl.ds(pl.multiple_of(gz * 16, 16), 16), :]
     for k in range(GZ - 1):
         v = v + rz[k]
@@ -362,6 +446,9 @@
         @pl.when(has[face])
         def _(face=face):
             z_copy(face).wait_send()
+            x_copy(face).wait_send()
+
+    mark(None)
 
 
 def call(pg, x, wp):
@@ -378,7 +465,7 @@
         out_specs=(vmem, vmem),
         scratch_shapes=[
             v((SX + 2, 3 * C, PROW), BF),
-            v(((SX + 4) * C, ROW), BF),
+            v((SX, 3 * C, ROW), BF),
             v((PROW, 2 * SZ), BF),
             v((2, SZ, PROW), BF),
             v((3, 3 * C, 2 * SZ), F32),
@@ -386,8 +473,8 @@
             v(((SX + 4) * C, ROW), F32),
             v((2, C, SZ), BF),
             v((2, C, SZ), BF),
-            v((2, C, SZ), F32),
-            v((2, 3 * C, SZ), BF),
+            v((2, C, SZ), BF),
+            v((2, C, SZ), BF),
             v((GZ - 1, 32, SZ), BF),
             v((GX, GY, 32, SZ), BF),
             v((1024, SZ), F32),
@@ -401,7 +488,7 @@
             v((GY - 1, 32, SZ), BF),
             v((SZ, SZ), F32),
             v((GZ - 1, 16, SZ), F32),
-            dma((8,)), dma((8,)), dma((2,)), dma((2,)),
+            dma((8,)), dma((8,)), dma((2,)), dma((2,)), dma((2,)), dma((2,)),
             dma((GZ - 1,)), dma((GZ - 1,)), dma((GY - 1,)), dma((GY - 1,)), dma((GX - 1,)), dma((GX - 1,)),
             dma((GX - 1,)), dma((GX - 1,)), dma((GY - 1,)), dma((GY - 1,)), dma((GZ - 1,)), dma((GZ - 1,)),
         ],

time: 57.4 us -> 51.4 us (0.90)
  Pallas kernels: 46 us -> 40 us
    pallas_call x1, Pallas kernels: 46 us -> 40 us  [call(): pl.pallas_call(kernel, out_shape=(jax.ShapeDtypeStruct((SX, C, ROW), BF),...]
where the time goes in v2:
time: 51.4 us; the launch traced here: 51.2 us
  Pallas kernels  40 us (78%)
  local copies, waits for them, and re-layouts  9.07 us (18%)
  other arithmetic  1.37 us (3%)
  between operations  0.77 us (1%)
    pallas_call x1, Pallas kernels, call(): pl.pallas_call(kernel, out_shape=(jax.ShapeDtypeStruct((SX, C, ROW), BF),...  40 us
    reshape x2, local copies, waits for them, and re-layouts, local(): x = jnp.transpose(activations, (1, 0, 2, 3)).reshape(SX, C, ROW)  3.07 us
    unnamed x15, local copies, waits for them, and re-layouts  2.77 us
    reshape x1, local copies, waits for them, and re-layouts, local(): jnp.transpose(pre_grad.reshape(C // 2, 2, SX, SY, SZ), (2, 1, 0, 3, 4))  1.27 us
    transpose x1, local copies, waits for them, and re-layouts, local(): grad_input = jnp.transpose(out.reshape(SX, C, SY, SZ), (1, 0, 2, 3))  1.27 us

profile of v2, /device:TPU:1, one launch (start us, length us, event | category | flops | bytes accessed | tf_op | source)
XLA Modules:
  0.0 51.2 jit_solution(16981381426810380009)
XLA Ops:
  0.6 0.0 copy-start.3
  0.7 0.7 %copy-done.3 = f32[432]{0:T(512)S(1)} copy-done((f32[432]{0:T(512)S(1)}, f32[432]{0:T(512)}, u32[]{:S(2)}) %copy-start.3) | copy-done | bytes 1752
  1.3 0.1 reshape.39
  1.4 0.1 copy.16
  1.5 0.6 %fusion.wp_ref = bf16[32,128]{1,0:T(8,128)(2,1)} fusion(bf16[32,128]{1,0:T(8,128)(2,1)S(1)} %copy.16, s32[]{:T(128)S(6)} %axis_index.12, s32[128]{0:T(128)S(1)} %get-tuple-element.15, s32[128]{0:T(128)S(1)} %get-tuple-element.16, pred[128]{0:T(512)(128)(4,1)S(1)} %compare_and_fusion), kind=kLoop, calls=%fused_computation.4 | loop fusion | flops 12288 | bytes 17540 | tf_op jit(solution)/shard_map/jit(_where)/select_n | solution.py:507
  2.1 1.5 %reshape.41 = bf16[8,64,1024]{2,0,1:T(8,128)(2,1)S(1)} reshape(bf16[8,64,8,128]{3,2,0,1:T(8,128)(2,1)} %bitcast.26) | data formatting | bytes 2097152 | tf_op jit(solution)/shard_map/reshape | solution.py:504
  3.7 0.0 copy-start
  3.7 0.0 copy-start.1
  3.7 1.6 %copy.18.x_ref = bf16[8,64,1024]{2,1,0:T(8,128)(2,1)} copy(bf16[8,64,1024]{2,0,1:T(8,128)(2,1)S(1)} %reshape.41) | data formatting | bytes 2097152 | tf_op jit(solution)/shard_map/reshape | solution.py:504
  5.2 0.0 copy-done
  5.2 0.0 copy-done.1
  5.3 0.1 compare_select_fusion
  5.4 0.3 copy.22
  5.6 1.3 %reshape.37.pg_ref = bf16[8,64,1024]{2,1,0:T(8,128)(2,1)} reshape(bf16[8,2,32,8,128]{4,3,2,1,0:T(8,128)(2,1)S(1)} %bitcast.24) | data formatting | bytes 2097152 | tf_op jit(solution)/shard_map/reshape | solution.py:503
  6.9 40.0 %shard_map.101 = (bf16[8,64,1024]{2,1,0:T(8,128)(2,1)}, f32[16,128]{1,0:T(8,128)}) custom-call(bf16[8,64,1024]{2,1,0:T(8,128)(2,1)} %reshape.37.pg_ref, bf16[8,64,1024]{2,1,0:T(8,128)(2,1)} %copy.18.x_ref, bf16[32,128]{1,0:T(8,128)(2,1)} %fusion.wp_ref), custom_call_target="tpu_custom_call" | custom-call | tf_op jit(solution)/shard_map/pallas_call | solution.py:458
  46.9 1.5 %copy.19 = bf16[64,8,8,128]{3,2,1,0:T(8,128)(2,1)S(1)} copy(bf16[64,8,8,128]{3,1,2,0:T(8,128)(2,1)} %bitcast.27) | data formatting | bytes 2097152
  48.4 0.0 copy-start.4
  48.4 1.3 %copy_bitcast_fusion = bf16[64,8,8,128]{3,2,1,0:T(8,128)(2,1)} fusion(bf16[8,64,8,128]{3,2,1,0:T(8,128)(2,1)S(1)} %bitcast.25), kind=kLoop, calls=%fused_computation.1 | loop fusion | bytes 2097152 | tf_op jit(solution)/shard_map/transpose | solution.py:509
  49.7 0.0 copy-done.4
  49.7 0.1 mul.54
  49.8 0.1 div.36
  49.9 0.0 copy-start.2
  49.9 0.0 copy-start.5
  49.9 0.0 copy-start.6
  49.9 0.1 mul.49
  50.0 0.5 copy-done.2
  50.5 0.1 copy-done.5
  50.6 0.0 copy-done.6
  50.6 0.6 %multiply_subtract_fusion = (f32[432]{0:T(512)}, f32[432]{0:T(512)}, f32[432]{0:T(512)}) fusion(f32[432]{0:T(512)S(1)} %copy-done.3, f32[432]{0:T(512)S(1)} %mul.49, f32[432]{0:T(512)S(1)} %copy-done.5, f32[432]{0:T(512)S(1)} %mul.54, f32[432]{0:T(512)S(1)} %div.36, f32[432]{0:T(512)S(1)} %copy-done.6), kind=kLoop, calls=%fused_computation.8 | loop fusion | flops 5616 | bytes 15552 | tf_op jit(solution)/shard_map/sub | solution.py:517
  (6 shorter events, 0.0 us)
Async XLA Ops:
  0.6 0.7 %copy-start.3 = (f32[432]{0:T(512)S(1)}, f32[432]{0:T(512)}, u32[]{:S(2)}) copy-start(f32[432]{0:T(512)} %param.9) | copy-start | bytes 5188
  3.7 1.6 %copy-start = (bf16[64,8,8,128]{3,2,1,0:T(8,128)(2,1)S(1)}, bf16[64,8,8,128]{3,2,1,0:T(8,128)(2,1)}, u32[]{:S(2)}) copy-start(bf16[64,8,8,128]{3,2,1,0:T(8,128)(2,1)} %param.8) | copy-start | bytes 3145732
  3.7 1.6 %copy-start.1 = (bf16[64,8,8,128]{3,2,1,0:T(8,128)(2,1)S(1)}, bf16[64,8,8,128]{3,2,1,0:T(8,128)(2,1)}, u32[]{:S(2)}) copy-start(bf16[64,8,8,128]{3,2,1,0:T(8,128)(2,1)} %param.7) | copy-start | bytes 3145732
  48.4 1.3 %copy-start.4 = (f32[16,128]{1,0:T(8,128)S(1)}, f32[16,128]{1,0:T(8,128)}, u32[]{:S(2)}) copy-start(f32[16,128]{1,0:T(8,128)} %get-tuple-element.8) | copy-start | bytes 24580
  49.9 0.6 %copy-start.2 = (f32[432]{0:T(512)}, f32[432]{0:T(512)S(1)}, u32[]{:S(2)}) copy-start(f32[432]{0:T(512)S(1)} %div.36) | copy-start | bytes 5188
  49.9 0.7 %copy-start.5 = (f32[432]{0:T(512)S(1)}, f32[432]{0:T(512)}, u32[]{:S(2)}) copy-start(f32[432]{0:T(512)} %param.10) | copy-start | bytes 5188
  49.9 0.7 %copy-start.6 = (f32[432]{0:T(512)S(1)}, f32[432]{0:T(512)}, u32[]{:S(2)}) copy-start(f32[432]{0:T(512)} %param.11) | copy-start | bytes 5188

commit v3 on v2

--- a/solution.py
+++ b/solution.py
@@ -17,6 +17,8 @@
 SX, SY, SZ = 8, 8, 128
 ROW = SY * SZ
 PROW = (SY + 2) * SZ
+NCH = 4
+CHUNK = C * SX * SY // NCH
 DIRS = [(1, 0), (-1, 0), (0, 1), (0, -1), (1, 1), (1, -1), (-1, 1), (-1, -1)]
 NT = (((1,), (1,)), ((), ()))
 NN = (((1,), (0,)), ((), ()))
@@ -42,7 +44,8 @@
 
 
 def kernel(
-    pg_ref, x_ref, wp_ref, out_ref, wg_ref,
+    pre_ref, up_ref, act_ref, m_ref, out_ref, wg_ref,
+    pbuf, ubuf, xbuf, nat, wt, wp_ref, in_s, out_s,
     pg3, x3, pack, spread, gacc, dfull, acc,
     zsend, zrecv, xsend, xrecv,
     az, ax, wf, wk, wl,
@@ -56,6 +59,16 @@
         return pltpu.make_async_remote_copy(
             src_ref=src, dst_ref=dst, send_sem=ss, recv_sem=rs, device_id=dev, device_id_type=MESH
         )
+
+    def fetch(src, dst, i, n):
+        at = pl.ds(i * CHUNK, CHUNK)
+        return pltpu.make_async_copy(src.at[at, :], dst.at[at, :], in_s.at[n, i])
+
+    for i in range(NCH):
+        fetch(pre_ref, pbuf, i, 0).start()
+        fetch(up_ref, ubuf, i, 1).start()
+    for i in range(NCH):
+        fetch(act_ref, xbuf, i, 2).start()
 
     mark("barsig")
     barrier = pltpu.get_barrier_semaphore()
@@ -74,22 +87,24 @@
         )
 
     mark("prep")
-    pg3[1 : SX + 1, C : 2 * C, SZ : SZ + ROW] = pg_ref[...]
+    wt[...] = jnp.zeros(wt.shape, F32)
+    wt[pl.ds(pl.multiple_of(gz * 16, 16), 16), 0:27] = m_ref[...]
+    wp_ref[...] = wt[...].T[0:32, :].astype(BF)
 
     def where(d):
         sxd, syd = d
         if sxd == 1:
-            sp, dp = pl.ds(SX - 1, 1), pl.ds(0, 1)
+            sp, dp = pl.ds(SX, 1), pl.ds(0, 1)
         elif sxd == -1:
-            sp, dp = pl.ds(0, 1), pl.ds(SX + 1, 1)
+            sp, dp = pl.ds(1, 1), pl.ds(SX + 1, 1)
         else:
-            sp, dp = pl.ds(0, SX), pl.ds(1, SX)
+            sp, dp = pl.ds(1, SX), pl.ds(1, SX)
         if syd == 1:
-            sl, dl = pl.ds(ROW - SZ, SZ), pl.ds(0, SZ)
+            sl, dl = pl.ds(ROW, SZ), pl.ds(0, SZ)
         elif syd == -1:
-            sl, dl = pl.ds(0, SZ), pl.ds(PROW - SZ, SZ)
+            sl, dl = pl.ds(SZ, SZ), pl.ds(PROW - SZ, SZ)
         else:
-            sl, dl = pl.ds(0, ROW), pl.ds(SZ, ROW)
+            sl, dl = pl.ds(SZ, ROW), pl.ds(SZ, ROW)
         return sp, sl, dp, dl
 
     def inside(dx, dy):
@@ -104,7 +119,7 @@
         if dy:
             dev["gy"] = gy + dy
         return send(
-            pg_ref.at[sp, :, sl], pg3.at[dp, pl.ds(C, C), dl], halo_s.at[k], halo_r.at[k], dev
+            pg3.at[sp, pl.ds(C, C), sl], pg3.at[dp, pl.ds(C, C), dl], halo_s.at[k], halo_r.at[k], dev
         )
 
     for k, (dx, dy) in enumerate(DIRS):
@@ -141,8 +156,56 @@
             zsend.at[face], zrecv.at[face], z_s.at[face], z_r.at[face], {"gz": gz + (1 - 2 * face)}
         )
 
+    mark("pgin")
+    for i in range(NCH):
+        fetch(pre_ref, pbuf, i, 0).wait()
+        fetch(up_ref, ubuf, i, 1).wait()
+
+        def select(r, carry, i=i):
+            at = pl.ds(pl.multiple_of(i * CHUNK + r * 128, 128), 128)
+            u = ubuf[at, :].astype(F32)
+            nat[at, :] = jnp.where(pbuf[at, :].astype(F32) > 0.0, u, 0.0)
+            return carry
+
+        lax.fori_loop(0, CHUNK // 128, select, 0)
+
+    def pgplane(i, carry):
+        for j in range(SY):
+            at = i * SY + j
+            to = pl.ds((j + 1) * SZ, SZ)
+            pg3[i + 1, C : C + C // 2, to] = nat[pl.ds(at, C // 2, stride=128), :].astype(BF)
+            pg3[i + 1, C + C // 2 : 2 * C, to] = nat[pl.ds(at + 64, C // 2, stride=128), :].astype(BF)
+        return carry
+
+    lax.fori_loop(0, SX, pgplane, 0)
+
+    mark("xin")
+    for i in range(NCH):
+        fetch(act_ref, xbuf, i, 2).wait()
+
+    def widen(r, carry):
+        at = pl.ds(pl.multiple_of(r * 128, 128), 128)
+        nat[at, :] = xbuf[at, :].astype(F32)
+        return carry
+
+    lax.fori_loop(0, C * SX * SY // 128, widen, 0)
+    lane = lanes((C, SZ))
+
+    def xplane(i, carry):
+        for j in range(SY):
+            t = nat[pl.ds(i * SY + j, C, stride=64), :]
+            up = jnp.where(lane == 0, 0.0, pltpu.roll(t, 1, 1))
+            down = jnp.where(lane == SZ - 1, 0.0, pltpu.roll(t, SZ - 1, 1))
+            x3[i, C : 2 * C, j * SZ : (j + 1) * SZ] = t.astype(BF)
+            x3[i, 0:C, j * SZ : (j + 1) * SZ] = up.astype(BF)
+            x3[i, 2 * C :, j * SZ : (j + 1) * SZ] = down.astype(BF)
+        return carry
+
+    lax.fori_loop(0, SX, xplane, 0)
+    gacc[...] = jnp.zeros(gacc.shape, F32)
+
     mark("xfaces")
-    high, low = faces(x_ref[...], 0)
+    high, low = faces(x3[:, C : 2 * C, :], 0)
     xsend[0] = high.astype(BF)
     xsend[1] = low.astype(BF)
 
@@ -168,22 +231,6 @@
 
     for k in range(1, GZ):
         send(wp_ref, az.at[k - 1], az_s.at[k - 1], az_r.at[k - 1], {"gz": lax.rem(gz + k, GZ)}).start()
-
-    mark("xshift")
-    lane = lanes((C, SZ))
-    gacc[...] = jnp.zeros(gacc.shape, F32)
-
-    def xshift(i, carry):
-        x3[i, C : 2 * C, :] = x_ref[i]
-        for j in range(SY):
-            t = x_ref[i, :, j * SZ : (j + 1) * SZ].astype(F32)
-            up = jnp.where(lane == 0, 0.0, pltpu.roll(t, 1, 1))
-            down = jnp.where(lane == SZ - 1, 0.0, pltpu.roll(t, SZ - 1, 1))
-            x3[i, 0:C, j * SZ : (j + 1) * SZ] = up.astype(BF)
-            x3[i, 2 * C :, j * SZ : (j + 1) * SZ] = down.astype(BF)
-        return carry
-
-    lax.fori_loop(0, SX, xshift, 0)
 
     CUT = ((256, 0, 896), (128, 0, 1024), (128, 128, 896))
 
@@ -423,8 +470,29 @@
 
     mark("dgrad2")
     lax.fori_loop(4, SX + 2, dgrad, 0)
-    for i in range(SX):
-        out_ref[i] = acc[(i + 2) * C : (i + 3) * C, :].astype(BF)
+    mark("out")
+
+    def oplane(i, carry):
+        at = pl.ds(pl.multiple_of((i + 2) * C, C), C)
+        for j in range(SY):
+            nat[pl.ds(i * SY + j, C, stride=64), :] = acc[at, j * SZ : (j + 1) * SZ]
+        return carry
+
+    lax.fori_loop(0, SX, oplane, 0)
+
+    def emit(i):
+        at = pl.ds(i * CHUNK, CHUNK)
+        return pltpu.make_async_copy(ubuf.at[at, :], out_ref.at[at, :], out_s.at[i])
+
+    for i in range(NCH):
+
+        def narrow(r, carry, i=i):
+            at = pl.ds(pl.multiple_of(i * CHUNK + r * 128, 128), 128)
+            ubuf[at, :] = nat[at, :].astype(BF)
+            return carry
+
+        lax.fori_loop(0, CHUNK // 128, narrow, 0)
+        emit(i).start()
 
     mark("rzwait")
     for k in range(1, GZ):
@@ -434,6 +502,8 @@
     for k in range(GZ - 1):
         v = v + rz[k]
     wg_ref[...] = v
+    for i in range(NCH):
+        emit(i).wait()
 
     for k, (dx, dy) in enumerate(DIRS):
 
@@ -451,19 +521,23 @@
     mark(None)
 
 
-def call(pg, x, wp):
+def call(pre, up, act, m):
     vmem = pl.BlockSpec(memory_space=pltpu.VMEM)
+    hbm = pl.BlockSpec(memory_space=pl.ANY)
     dma = pltpu.SemaphoreType.DMA
     v = pltpu.VMEM
+    n = C * SX * SY
     return pl.pallas_call(
         kernel,
         out_shape=(
-            jax.ShapeDtypeStruct((SX, C, ROW), BF),
+            jax.ShapeDtypeStruct((n, SZ), BF),
             jax.ShapeDtypeStruct((16, SZ), F32),
         ),
-        in_specs=[vmem] * 3,
-        out_specs=(vmem, vmem),
+        in_specs=[hbm, hbm, hbm, vmem],
+        out_specs=(hbm, vmem),
         scratch_shapes=[
+            v((n, SZ), BF), v((n, SZ), BF), v((n, SZ), BF), v((n, SZ), F32),
+            v((SZ, SZ), F32), v((32, SZ), BF), dma((3, NCH)), dma((NCH,)),
             v((SX + 2, 3 * C, PROW), BF),
             v((SX, 3 * C, ROW), BF),
             v((PROW, 2 * SZ), BF),
@@ -495,18 +569,13 @@
         compiler_params=pltpu.CompilerParams(
             collective_id=0, has_side_effects=True, vmem_limit_bytes=56 * 1024 * 1024
         ),
-    )(pg, x, wp)
+    )(pre, up, act, m)
 
 
 def local(activations, preact, upstream, master, first_moment, second_moment):
-    pre_grad = jnp.where(preact > 0, upstream, jnp.zeros_like(upstream))
-    pg = jnp.transpose(pre_grad.reshape(C // 2, 2, SX, SY, SZ), (2, 1, 0, 3, 4)).reshape(SX, C, ROW)
-    x = jnp.transpose(activations, (1, 0, 2, 3)).reshape(SX, C, ROW)
-    w = jnp.pad(master.astype(BF).reshape(16, 27).T, ((0, 5), (0, 0)))
-    own = lax.broadcasted_iota(jnp.int32, (32, SZ), 1) // 16 == lax.axis_index("gz")
-    wp = jnp.where(own, jnp.tile(w, (1, 8)), jnp.zeros((), BF))
-    out, wg = call(pg, x, wp)
-    grad_input = jnp.transpose(out.reshape(SX, C, SY, SZ), (1, 0, 2, 3))
+    flat = [v.reshape(C * SX * SY, SZ) for v in (preact, upstream, activations)]
+    out, wg = call(*flat, master.reshape(16, 27))
+    grad_input = out.reshape(C, SX, SY, SZ)
     voxels = SX * SY * SZ * GX * GY * GZ
     weight_grad = wg[:, :27].reshape(-1) / math.sqrt(voxels)
     new_first = 0.9 * first_moment + 0.1 * weight_grad

time: 51.4 us -> 48.1 us (0.936)
  local copies, waits for them, and re-layouts: 9.07 us -> 4.48 us
  Pallas kernels: 40 us -> 41.4 us
    reshape x5 -> x1, local copies, waits for them, and re-layouts: 4.69 us -> 0.69 us  [local(): out, wg = call(*flat, master.reshape(16, 27))]
    pallas_call x1, Pallas kernels: 40 us -> 41.4 us  [call(): pl.pallas_call(kernel, out_shape=(jax.ShapeDtypeStruct((n, SZ), BF), jax....]
    transpose x1 -> x0, local copies, waits for them, and re-layouts: 1.27 us -> none  [local(): grad_input = jnp.transpose(out.reshape(SX, C, SY, SZ), (1, 0, 2, 3))]
    unnamed x15 -> x9, local copies, waits for them, and re-layouts: 2.77 us -> 3.54 us
    select_n x2 -> x0, other arithmetic: 0.74 us -> none  [the longest x1 0.63 us: local(): wp = jnp.where(own, jnp.tile(w, (1, 8)), jnp.zeros((), BF))]
    mul x1, other arithmetic: 0.01 us -> 0.7 us  [local(): new_second = 0.999 * second_moment + 0.001 * weight_grad * weight_grad]
where the time goes in v3:
time: 48.1 us; the launch traced here: 47.9 us
  Pallas kernels  41.4 us (86%)
  local copies, waits for them, and re-layouts  4.48 us (9%)
  other arithmetic  1.3 us (3%)
  between operations  0.68 us (1%)
    pallas_call x1, Pallas kernels, call(): pl.pallas_call(kernel, out_shape=(jax.ShapeDtypeStruct((n, SZ), BF), jax....  41.4 us
    unnamed x9, local copies, waits for them, and re-layouts  3.54 us

profile of v3, /device:TPU:1, one launch (start us, length us, event | category | flops | bytes accessed | tf_op | source)
XLA Modules:
  0.0 47.9 jit_solution(14382905926490229218)
XLA Ops:
  0.6 0.0 copy-start
  0.6 0.7 %copy-done = f32[432]{0:T(512)S(1)} copy-done((f32[432]{0:T(512)S(1)}, f32[432]{0:T(512)}, u32[]{:S(2)}) %copy-start) | copy-done | bytes 1752
  1.3 0.7 %reshape.35.m_ref = f32[16,27]{1,0:T(8,128)} reshape(f32[432]{0:T(512)S(1)} %copy-done) | data formatting | bytes 3456 | tf_op jit(solution)/shard_map/reshape | solution.py:577
  2.0 41.4 %shard_map.101 = (bf16[4096,128]{1,0:T(8,128)(2,1)}, f32[16,128]{1,0:T(8,128)}) custom-call(bf16[4096,128]{1,0:T(8,128)(2,1)} %bitcast.4, bf16[4096,128]{1,0:T(8,128)(2,1)} %bitcast.5, bf16[4096,128]{1,0:T(8,128)(2,1)} %bitcast.6, f32[16,27]{1,0:T(8,128)} %reshape.35.m_ref), custom_call_target="tpu_custom_call" | custom-call | tf_op jit(solution)/shard_map/pallas_call | solution.py:530
  43.4 0.7 %slice_multiply_fusion = (f32[16,27]{1,0:T(8,128)S(1)}, f32[16,27]{1,0:T(8,128)S(1)}, f32[16,27]{1,0:T(8,128)S(1)}) fusion(f32[16,128]{1,0:T(8,128)} %get-tuple-element.8), kind=kLoop, calls=%fused_computation | loop fusion | flops 1296 | bytes 6912 | tf_op jit(solution)/shard_map/mul | solution.py:582
  44.1 0.1 mul.54
  44.2 0.1 div.25
  44.3 0.0 copy-start.1
  44.3 0.0 copy-start.2
  44.3 0.0 copy-start.3
  44.3 0.1 mul.49
  44.4 0.5 copy-done.1
  44.9 0.1 copy-done.2
  45.0 0.0 copy-done.3
  45.0 0.6 %multiply_subtract_fusion = (f32[432]{0:T(512)}, f32[432]{0:T(512)}, f32[432]{0:T(512)}) fusion(f32[432]{0:T(512)S(1)} %copy-done, f32[432]{0:T(512)S(1)} %mul.49, f32[432]{0:T(512)S(1)} %copy-done.2, f32[432]{0:T(512)S(1)} %mul.54, f32[432]{0:T(512)S(1)} %div.25, f32[432]{0:T(512)S(1)} %copy-done.3), kind=kLoop, calls=%fused_computation.3 | loop fusion | flops 5616 | bytes 15552 | tf_op jit(solution)/shard_map/sub | solution.py:586
  45.6 2.3 %copy.12 = bf16[64,8,8,128]{3,2,1,0:T(8,128)(2,1)} copy(bf16[64,8,8,128]{3,2,1,0:T(8,128)(2,1)} %bitcast.7) | data formatting | bytes 2097152
Async XLA Ops:
  0.6 0.7 %copy-start = (f32[432]{0:T(512)S(1)}, f32[432]{0:T(512)}, u32[]{:S(2)}) copy-start(f32[432]{0:T(512)} %param.9) | copy-start | bytes 5188
  44.3 0.6 %copy-start.1 = (f32[432]{0:T(512)}, f32[432]{0:T(512)S(1)}, u32[]{:S(2)}) copy-start(f32[432]{0:T(512)S(1)} %div.25) | copy-start | bytes 5188
  44.3 0.7 %copy-start.2 = (f32[432]{0:T(512)S(1)}, f32[432]{0:T(512)}, u32[]{:S(2)}) copy-start(f32[432]{0:T(512)} %param.10) | copy-start | bytes 5188
  44.3 0.7 %copy-start.3 = (f32[432]{0:T(512)S(1)}, f32[432]{0:T(512)}, u32[]{:S(2)}) copy-start(f32[432]{0:T(512)} %param.11) | copy-start | bytes 5188
